TPU v7x, 32 devices: a whole 2x2x4 slice. The times are simulated.
32 devices in a mesh: dp: 4 (over z), tensor: 4 (over y, x), pipe: 2 (over core).
Axes of the slice: x: 2, y: 2, z: 4, core: 2. Of those that a mesh axis runs over, the one named last changes fastest.
Arguments:
- patches: bfloat16 [1280, 3072], P('tensor', ('dp', 'pipe')), may hold values from -6 to 6
- lengths: int32 [384], P(('dp', 'pipe')), may hold values from 1 to 8
- slot_plan: int32 [384], P(('dp', 'pipe')), may hold values from 0 to 47, as said below
- starts: int32 [384], P(('dp', 'pipe')), may hold values from 0 to 564, as said below
- text_rows: bfloat16 [1280, 4608], P('tensor', ('dp', 'pipe')), may hold values from -6 to 6
- cotangent: bfloat16 [1280, 4608], P('tensor', ('dp', 'pipe')), may hold values from -6 to 6
- ln_gain: float32 [1280], replicated, may hold values from 0.25 to 1.75
- ln_bias: float32 [1280], replicated, may hold values from -3 to 3
- w_qkv: bfloat16 [3, 1280, 1280], P(None, 'tensor'), may hold values from -0.15625 to 0.15625
- w_out: bfloat16 [1280, 1280], P('tensor'), may hold values from -0.15625 to 0.15625
Outputs:
- features: bfloat16 [1280, 4608], P('tensor', ('dp', 'pipe'))
- weight_grad: float32 [1280, 1280], P('tensor', ('dp', 'pipe'))
Inputs may be any that keep to these rules, and one draw needn't show every extreme that they name: `slot_plan`: the 48 images of one data group have distinct slots. `starts`: within each data group the 48 places' blocks of 8 positions rise and are disjoint, separated by 0 to 4 positions, and lie inside the group's 576 positions.
All inputs are finite; a program needn't handle non-finite values.
Results may differ from a plain program's by a relative error of at most 0.0073.
Values may be sent and summed in bfloat16 or wider, within the bound.
No kernel may reach another device: no remote copies, remote signals or barrier semaphores. Data moves between devices by JAX's collectives and lax.ppermute only.
A program may use at most 64 MiB of HBM per device.

v0:
```python
import math

import jax
import jax.numpy as jnp
from jax import lax
from jax.experimental import pallas as pl
from jax.experimental.pallas import tpu as pltpu
from jax.sharding import PartitionSpec as P

HEAD_DIM = 80


epsilon = 1e-06


def shards_any(
    patches, lengths, slot_plan, starts, text_rows, cotangent, ln_gain, ln_bias, w_qkv, w_out
):
    cols_here, flat_count = patches.shape
    image_count = lengths.shape[0]
    length = flat_count // image_count
    groups = lax.axis_size("dp")
    capacity = (image_count + groups - 1) // groups
    slot_total = groups * capacity
    heads_here = w_qkv.shape[1] // HEAD_DIM
    seq_rows = text_rows.shape[1]
    slot_ids = jnp.arange(slot_total, dtype=jnp.int32)
    picker = (slot_ids[:, None] == slot_plan[None, :]).astype(jnp.bfloat16)
    stacked = patches.reshape(cols_here, image_count, length)
    outgoing = jnp.einsum("si,cil->scl", picker, stacked, preferred_element_type=jnp.float32)
    outgoing = outgoing.astype(jnp.bfloat16).reshape(groups, capacity * cols_here * length)
    sizes_out = jnp.dot(
        picker, lengths.astype(jnp.bfloat16)[:, None], preferred_element_type=jnp.float32
    )
    sizes_out = sizes_out.astype(jnp.bfloat16).reshape(groups, capacity)
    arrived, sizes_in = (
        lax.all_to_all(outgoing, "dp", split_axis=0, concat_axis=0, tiled=True),
        lax.all_to_all(sizes_out, "dp", split_axis=0, concat_axis=0, tiled=True),
    )
    live_len = sizes_in.reshape(slot_total).astype(jnp.int32)
    own_rows = (
        arrived.reshape(slot_total, cols_here, length)
        .transpose(1, 0, 2)
        .reshape(cols_here, slot_total * length)
    )
    offsets = jnp.arange(length, dtype=jnp.int32)
    patch_pos = jnp.minimum(starts[:, None] + offsets[None, :], seq_rows - 1).reshape(-1)
    own_cot = cotangent[:, patch_pos]
    full_rows, cot_patch = (
        lax.all_gather(own_rows, "tensor", axis=0, tiled=True),
        lax.all_gather(own_cot, "tensor", axis=0, tiled=True),
    )
    inputs_f = full_rows.astype(jnp.float32)
    average = jnp.mean(inputs_f, axis=0, keepdims=True)
    centred = inputs_f - average
    variance = jnp.mean(centred * centred, axis=0, keepdims=True)
    normed = (centred * lax.rsqrt(variance + epsilon) * ln_gain[:, None] + ln_bias[:, None]).astype(
        jnp.bfloat16
    )
    shape_heads = (heads_here, HEAD_DIM, slot_total, length)
    queries = (
        jnp.dot(w_qkv[0], normed, preferred_element_type=jnp.float32)
        .astype(jnp.bfloat16)
        .reshape(shape_heads)
    )
    key_rows = (
        jnp.dot(w_qkv[1], normed, preferred_element_type=jnp.float32)
        .astype(jnp.bfloat16)
        .reshape(shape_heads)
    )
    value_rows = (
        jnp.dot(w_qkv[2], normed, preferred_element_type=jnp.float32)
        .astype(jnp.bfloat16)
        .reshape(shape_heads)
    )
    scores = jnp.einsum("hesq,hesk->hsqk", queries, key_rows, preferred_element_type=jnp.float32)
    scores = scores * (1.0 / math.sqrt(HEAD_DIM))
    key_live = offsets[None, :] < jnp.maximum(live_len, 1)[:, None]
    scores = jnp.where(key_live[None, :, None, :], scores, -1e30)
    top = jnp.max(scores, axis=-1, keepdims=True)
    raised = jnp.exp(scores - top)
    weights = (raised / jnp.sum(raised, axis=-1, keepdims=True)).astype(jnp.bfloat16)
    context = jnp.einsum(
        "hsqk,hesk->hesq", weights, value_rows, preferred_element_type=jnp.float32
    ).astype(jnp.bfloat16)
    query_live = offsets[None, :] < live_len[:, None]
    context = jnp.where(query_live[None, None, :, :], context, jnp.zeros_like(context))
    context = context.reshape(heads_here * HEAD_DIM, slot_total * length)
    head_terms = lax.dot_general(
        w_out, context, (((0,), (0,)), ((), ())), preferred_element_type=jnp.float32
    )
    attended = lax.psum_scatter(
        head_terms.astype(jnp.bfloat16), "tensor", scatter_dimension=0, tiled=True
    )
    merged = (own_rows.astype(jnp.float32) + attended.astype(jnp.float32)).astype(jnp.bfloat16)
    positions = jnp.arange(seq_rows, dtype=jnp.int32)[:, None]
    covered = (positions >= starts[None, :]) & (positions < starts[None, :] + live_len[None, :])
    source = jnp.sum(
        jnp.where(covered, slot_ids[None, :] * length + positions - starts[None, :], 0), axis=1
    )
    placed = merged[:, source]
    features = jnp.where(jnp.any(covered, axis=1)[None, :], placed, text_rows)
    grad_terms = lax.dot_general(
        context, cot_patch, (((1,), (1,)), ((), ())), preferred_element_type=jnp.float32
    )
    weight_grad = lax.psum_scatter(grad_terms, ("dp", "pipe"), scatter_dimension=1, tiled=True)
    return (features, weight_grad)


LANES = 128
NN = (((1,), (0,)), ((), ()))
NT = (((1,), (1,)), ((), ()))
TN = (((0,), (0,)), ((), ()))


def mm(left, right, dims=NN):
    return lax.dot_general(left, right, dims, preferred_element_type=jnp.float32)


def iota(shape, axis):
    return lax.broadcasted_iota(jnp.int32, shape, axis)


def onehot(condition):
    return jnp.where(condition, 1.0, 0.0).astype(jnp.bfloat16)


class Plan:
    def __init__(self, mesh, patches, lengths, text_rows, w_qkv):
        self.dp, self.tensor, self.pipe = (mesh.shape[name] for name in ("dp", "tensor", "pipe"))
        self.cols, self.flat = patches.shape
        self.images = lengths.shape[0]
        self.length = self.flat // self.images
        self.shift = self.length.bit_length() - 1
        self.capacity = (self.images + self.dp - 1) // self.dp
        self.slots = self.dp * self.capacity
        self.seq = text_rows.shape[1]
        self.width = w_qkv.shape[2]
        self.heads = w_qkv.shape[1] // HEAD_DIM
        self.block = self.capacity * self.length
        self.rest = LANES - self.block
        self.out = self.width // (self.dp * self.pipe)

    def packed(self):
        powers = all(n & (n - 1) == 0 for n in (self.dp, self.tensor, self.length))
        if not powers or self.pipe != 2 or self.dp > 8 or self.tensor > 8:
            return False
        if self.rest <= 0 or self.block % self.rest or self.images != self.slots:
            return False
        if self.flat % LANES or self.width % LANES or self.slots > 256 or self.seq > 4096 or self.width != self.cols * self.tensor:
            return False
        self.parts = self.block // self.rest
        if self.cols % ((self.parts + 1) * 16) or LANES % self.length:
            return False
        self.extra = self.cols // (self.parts + 1)
        self.main = self.extra * self.parts
        self.whole, last = divmod(self.cols, LANES)
        if last == 0 or LANES % last or self.out % (LANES // last * 16):
            return False
        self.pieces = LANES // last
        self.fold = self.out // self.pieces
        self.tall = self.whole * self.out + self.fold
        return self.heads * HEAD_DIM == self.cols


def spread(row, picker):
    wide = jnp.broadcast_to(row.astype(jnp.float32), (8, row.shape[1])).astype(jnp.bfloat16)
    return mm(wide, picker)[0:1]


def pack_kernel(plan, slot_ref, length_ref, start_ref, patches_ref, cot_ref, *refs):
    outs, cot_out, pos_out, rows = refs[: plan.dp], refs[plan.dp], refs[plan.dp + 1], refs[plan.dp + 2]
    mine = lax.axis_index("dp")
    flat, shift, block = plan.flat, plan.shift, plan.block
    lane = iota((1, flat), 1)
    inner = lane & (plan.length - 1)
    by_image = onehot(iota((plan.images, flat), 0) == (iota((plan.images, flat), 1) >> shift))
    target = spread(slot_ref[...], by_image).astype(jnp.int32) * plan.length + inner
    rows[: plan.main] = patches_ref[: plan.main]
    size_row = spread(length_ref[...], by_image)
    rows[plan.main :] = jnp.broadcast_to(size_row, (16, flat)).astype(jnp.bfloat16)
    extra = patches_ref[plan.main :]
    at = iota((LANES, flat), 0)
    for step in range(plan.dp):
        offset = target - (mine ^ step) * block
        straight = onehot((at < block) & (at == offset))
        outs[step][...] = mm(rows[...], straight, NT).astype(jnp.bfloat16)
        for part in range(plan.parts):
            turned = onehot((at >= block) & (at - block + part * plan.rest == offset))
            here = pl.ds(part * plan.extra, plan.extra)
            both = mm(extra, turned, NT) + outs[step][here].astype(jnp.float32)
            outs[step][here] = both.astype(jnp.bfloat16)
    full_lane = iota((plan.slots, flat), 1)
    order = jnp.zeros((plan.slots, flat), jnp.int32)
    for step in range(1, plan.dp):
        order = order + jnp.where(full_lane >= step * block, 1, 0)
    place = (order ^ mine) * plan.capacity + ((full_lane - order * block) >> shift)
    by_place = onehot(iota((plan.slots, flat), 0) == place)
    starts = start_ref[...]
    high, low = spread(starts >> 4, by_place), spread(starts & 15, by_place)
    position = (high * 16.0 + low).astype(jnp.int32) + inner
    pos_out[...] = jnp.broadcast_to(position, (8, flat))
    chosen = onehot(iota((plan.seq, flat), 0) == position)
    cot_out[...] = mm(cot_ref[...], chosen).astype(jnp.bfloat16)


def unpack_kernel(plan, *refs):
    blocks, own_out, size_out, wide = refs[: plan.dp], refs[plan.dp], refs[plan.dp + 1], refs[plan.dp + 2]
    for step in range(plan.dp):
        wide[:, step * LANES : (step + 1) * LANES] = blocks[step][...]
    shape = (plan.dp * LANES, plan.flat)
    source, column = iota(shape, 0), iota(shape, 1)
    step, lane = source >> 7, source & (LANES - 1)
    goal = step * plan.block + lane
    straight = onehot((lane < plan.block) & (column == goal))
    plain = mm(wide[...], straight).astype(jnp.bfloat16)
    own_out[: plan.main] = plain[: plan.main]
    size_out[...] = plain[plan.main :]
    extra = None
    for part in range(plan.parts):
        turned = onehot((lane >= plan.block) & (column == goal - plan.block + part * plan.rest))
        term = mm(wide[part * plan.extra : (part + 1) * plan.extra], turned)
        extra = term if extra is None else extra + term
    own_out[plan.main :] = extra.astype(jnp.bfloat16)


def prepare_kernel(plan, gain_ref, bias_ref, qkv_hbm, out_ref, qkv_out, turned_out, affine, done):
    copy = pltpu.make_async_copy(qkv_hbm, qkv_out, done)
    copy.start()
    for chunk in range(plan.width // LANES):
        here = slice(chunk * LANES, (chunk + 1) * LANES)
        for kind, vector_ref in enumerate((gain_ref, bias_ref)):
            row = jnp.broadcast_to(vector_ref[chunk : chunk + 1], (8, LANES))
            affine[kind, here] = jnp.transpose(row)
        turned_out[here] = jnp.transpose(out_ref[:, here])
    copy.wait()


def attend_kernel(plan, *refs):
    blocks = refs[: plan.tensor]
    size_ref, affine, qkv_ref, turned_ref = refs[plan.tensor : plan.tensor + 4]
    context_out = refs[plan.tensor + 4]
    terms_out = refs[plan.tensor + 5 : 2 * plan.tensor + 5]
    full, normed, qkv = refs[2 * plan.tensor + 5 :]
    mine = lax.axis_index("tensor")
    cols = plan.cols
    for step in range(plan.tensor):
        here = pl.multiple_of((mine ^ step) * cols, 16)
        full[pl.ds(here, cols)] = blocks[step][...]
    gain, bias = affine[0, :, 0:1], affine[1, :, 0:1]
    rows = full[...].astype(jnp.float32)
    average = jnp.sum(rows, axis=0, keepdims=True) / plan.width
    centred = rows - average
    variance = jnp.sum(centred * centred, axis=0, keepdims=True) / plan.width
    normed[...] = (centred * lax.rsqrt(variance + epsilon) * gain + bias).astype(jnp.bfloat16)
    for kind in range(3):
        qkv[kind] = mm(qkv_ref[kind], normed[...]).astype(jnp.bfloat16)
    key_at, query_at = iota((LANES, LANES), 0), iota((LANES, LANES), 1)
    same = (key_at >> plan.shift) == (query_at >> plan.shift)
    key_inner = key_at & (plan.length - 1)
    query_inner = iota((1, LANES), 1) & (plan.length - 1)
    scale = 1.0 / math.sqrt(HEAD_DIM)
    for group in range(plan.flat // LANES):
        columns = slice(group * LANES, (group + 1) * LANES)
        size = size_ref[0:1, columns].astype(jnp.float32).astype(jnp.int32)
        live = same & (key_inner < jnp.maximum(size, 1))
        for head in range(plan.heads):
            features = slice(head * HEAD_DIM, (head + 1) * HEAD_DIM)
            scores = mm(qkv[1, features, columns], qkv[0, features, columns], TN) * scale
            scores = jnp.where(live, scores, -1e30)
            top = jnp.max(scores, axis=0, keepdims=True)
            raised = jnp.exp(scores - top)
            weights = (raised / jnp.sum(raised, axis=0, keepdims=True)).astype(jnp.bfloat16)
            context = mm(qkv[2, features, columns], weights)
            context = jnp.where(query_inner < size, context, 0.0)
            context_out[features, columns] = context.astype(jnp.bfloat16)
    for step in range(plan.tensor):
        here = pl.multiple_of((mine ^ step) * cols, 16)
        terms_out[step][...] = mm(turned_ref[pl.ds(here, cols)], context_out[...]).astype(jnp.bfloat16)


def place_kernel(plan, *refs):
    terms = refs[: plan.tensor]
    own_ref, size_ref, pos_ref, text_ref, features_out = refs[plan.tensor :]
    total = terms[0][...].astype(jnp.float32)
    for term in terms[1:]:
        total = total + term[...].astype(jnp.float32)
    attended = total.astype(jnp.bfloat16).astype(jnp.float32)
    merged = (own_ref[...].astype(jnp.float32) + attended).astype(jnp.bfloat16)
    inner = iota((1, plan.flat), 1) & (plan.length - 1)
    size = size_ref[0:1].astype(jnp.float32).astype(jnp.int32)
    position = jnp.where(inner < size, pos_ref[0:1], -1)
    chosen = onehot(iota((plan.seq, plan.flat), 0) == position)
    placed = mm(merged, chosen, NT).astype(jnp.bfloat16)
    covered = mm(jnp.ones((8, plan.flat), jnp.bfloat16), chosen, NT)[0:1]
    features_out[...] = jnp.where(covered > 0.5, placed, text_ref[...])


def grad_kernel(plan, context_ref, *refs):
    blocks = refs[: plan.tensor]
    keep_out, send_out, full, turned = refs[plan.tensor :]
    place, mine, core = lax.axis_index("dp"), lax.axis_index("tensor"), lax.axis_index("pipe")
    cols, whole, out, fold = plan.cols, plan.whole, plan.out, plan.fold
    for step in range(plan.tensor):
        here = pl.multiple_of((mine ^ step) * cols, 16)
        full[pl.ds(here, cols)] = blocks[step][...]
    last = plan.cols - whole * LANES
    turned[...] = jnp.zeros_like(turned)
    for piece in range(plan.pieces):
        turned[piece, piece * last : (piece + 1) * last] = context_ref[whole * LANES :]
    for step in range(plan.dp):
        for other in range(2):
            target = send_out if other else keep_out
            first = pl.multiple_of(((place ^ step) * 2 + (core ^ other)) * out, 16)
            for index in range(whole):
                part = context_ref[index * LANES : (index + 1) * LANES]
                value = mm(full[pl.ds(first, out)], part, NT)
                target[step, index * out : (index + 1) * out] = value.astype(target.dtype)
            value = None
            for piece in range(plan.pieces):
                term = mm(full[pl.ds(first + piece * fold, fold)], turned[piece], NT)
                value = term if value is None else value + term
            target[step, whole * out :] = value.astype(target.dtype)


def pair_kernel(plan, keep_ref, came_ref, own_out, *outs):
    own_out[...] = keep_ref[0] + came_ref[0].astype(jnp.float32)
    for step in range(1, plan.dp):
        total = keep_ref[step] + came_ref[step].astype(jnp.float32)
        outs[step - 1][...] = total.astype(jnp.bfloat16)


def sum_kernel(plan, own_ref, *refs):
    grad_out, total = refs[-2:]
    value = own_ref[...]
    for term in refs[:-2]:
        value = value + term[...].astype(jnp.float32)
    total[...] = value
    whole, out, fold = plan.whole, plan.out, plan.fold
    last = plan.cols - whole * LANES
    for index in range(whole):
        grad_out[:, index * LANES : (index + 1) * LANES] = total[index * out : (index + 1) * out]
    for piece in range(plan.pieces):
        part = total[whole * out :, piece * last : (piece + 1) * last]
        grad_out[piece * fold : (piece + 1) * fold, whole * LANES :] = part


VMEM = pl.BlockSpec(memory_space=pltpu.VMEM)


def call(body, plan, outs, scratch, *operands, space, cost, specs=None):
    def kernel(*refs):
        body(plan, *refs)

    return pl.pallas_call(
        kernel,
        out_shape=[jax.ShapeDtypeStruct(shape, kind) for shape, kind in outs],
        in_specs=specs or [VMEM] * len(operands),
        out_specs=[VMEM] * len(outs),
        scratch_shapes=scratch,
        compiler_params=pltpu.CompilerParams(vmem_limit_bytes=space << 20),
        cost_estimate=pl.CostEstimate(flops=0, bytes_accessed=cost << 20, transcendentals=0),
    )(*operands)


def swap(value, axis, step):
    count = lax.axis_size(axis)
    return lax.ppermute(value, axis, [(index, index ^ step) for index in range(count)])


def shards_packed(
    plan, patches, lengths, slot_plan, starts, text_rows, cotangent, ln_gain, ln_bias, w_qkv, w_out
):
    half, single = jnp.bfloat16, jnp.float32
    cols, flat, width = plan.cols, plan.flat, plan.width
    height, tall = plan.main + 16, plan.tall
    packed = call(
        pack_kernel, plan,
        [((height, LANES), half)] * plan.dp + [((cols, flat), half), ((8, flat), jnp.int32)],
        [pltpu.VMEM((height, flat), half)],
        slot_plan[None], lengths[None], starts[None], patches, cotangent,
        space=8, cost=3,
    )
    blocks, own_cot, positions = packed[: plan.dp], packed[plan.dp], packed[plan.dp + 1]
    arrived = [blocks[0]] + [swap(blocks[step], "dp", step) for step in range(1, plan.dp)]
    cots = [own_cot] + [swap(own_cot, "tensor", step) for step in range(1, plan.tensor)]
    own_rows, sizes = call(
        unpack_kernel, plan,
        [((cols, flat), half), ((16, flat), half)],
        [pltpu.VMEM((height, plan.dp * LANES), half)],
        *arrived, space=6, cost=3,
    )
    rows = [own_rows] + [swap(own_rows, "tensor", step) for step in range(1, plan.tensor)]
    qkv, turned, affine = call(
        prepare_kernel, plan,
        [(w_qkv.shape, half), ((width, cols), half), ((2, width, 8), single)],
        [pltpu.SemaphoreType.DMA],
        ln_gain.reshape(-1, LANES), ln_bias.reshape(-1, LANES), w_qkv, w_out,
        space=10, cost=6,
        specs=[VMEM, VMEM, pl.BlockSpec(memory_space=pltpu.HBM), VMEM],
    )
    attended = call(
        attend_kernel, plan,
        [((cols, flat), half)] * (1 + plan.tensor),
        [
            pltpu.VMEM((width, flat), half),
            pltpu.VMEM((width, flat), half),
            pltpu.VMEM((3, cols, flat), half),
        ],
        *rows, sizes, affine, qkv, turned, space=24, cost=12,
    )
    context, terms = attended[0], attended[1:]
    came = [terms[0]] + [swap(terms[step], "tensor", step) for step in range(1, plan.tensor)]
    keep, send = call(
        grad_kernel, plan,
        [((plan.dp, tall, LANES), single), ((plan.dp, tall, LANES), half)],
        [pltpu.VMEM((width, flat), half), pltpu.VMEM((plan.pieces, LANES, flat), half)],
        context, *cots, space=10, cost=6,
    )
    pair = call(
        pair_kernel, plan,
        [((tall, LANES), single)] + [((tall, LANES), half)] * (plan.dp - 1),
        [],
        keep, swap(send, "pipe", 1), space=6, cost=3,
    )
    sums = [swap(pair[step], "dp", step) for step in range(1, plan.dp)]
    (weight_grad,) = call(
        sum_kernel, plan, [((plan.out, cols), single)], [pltpu.VMEM((tall, LANES), single)],
        pair[0], *sums, space=4, cost=2,
    )
    (features,) = call(
        place_kernel, plan, [((cols, plan.seq), half)], [],
        *came, own_rows, sizes, positions, text_rows, space=6, cost=4,
    )
    return (features, weight_grad.T)


def solution(mesh):
    placed = (
        P("tensor", ("dp", "pipe")),
        P(("dp", "pipe")),
        P(("dp", "pipe")),
        P(("dp", "pipe")),
        P("tensor", ("dp", "pipe")),
        P("tensor", ("dp", "pipe")),
        P(),
        P(),
        P(None, "tensor", None),
        P("tensor", None),
    )

    def shards(*arrays):
        plan = Plan(mesh, arrays[0], arrays[1], arrays[4], arrays[8])
        if not plan.packed():
            return shards_any(*arrays)
        return shards_packed(plan, *arrays)

    return jax.shard_map(
        shards,
        mesh=mesh,
        in_specs=placed,
        out_specs=(P("tensor", ("dp", "pipe")), P("tensor", ("dp", "pipe"))),
        check_vma=False,
    )
```

profile of v0, /device:TPU:0, one launch (start us, length us, event | category | flops | bytes accessed | tf_op | source)
XLA Modules:
  0.0 60.8 jit_solution(1416520788256136345)
XLA Ops:
  4.5 1.3 %shard_map.113 = (bf16[256,128]{1,0:T(8,128)(2,1)S(1)}, bf16[256,128]{1,0:T(8,128)(2,1)S(1)}, bf16[256,128]{1,0:T(8,128)(2,1)S(1)}, bf16[256,128]{1,0:T(8,128)(2...) custom-call(s32[1,48]{1,0:T(1,128)S(1)} %bitcast.8, s32[1,48]{1,0:T(1,128)S(1)} %bitcast.9, ...), custom_call_target="tpu_custom_call" | custom-call | bytes 3145728 | tf_op jit(solution)/shard_map/pallas_call | solution.py:355
  5.9 3.1 %collective-permute-start = (bf16[256,128]{1,0:T(8,128)(2,1)S(1)}, bf16[256,128]{1,0:T(8,128)(2,1)S(1)}, u32[]{:S(2)}, u32[]{:S(2)}) collective-permute-start(bf16[256,128]{1,0:T(8,128)(2,1)S(1)} %get-tuple-element.25), channel_id=1, source_target_pairs={{0,8},{8,0},{16,24},{24,16},{1,9},{9,1},{17,25},{25,17},{2,10},{10... | collective-permute-start | bytes 196616 | tf_op jit(solution)/shard_map/ppermute | solution.py:368
  9.0 2.6 %collective-permute-start.1 = (bf16[256,128]{1,0:T(8,128)(2,1)S(1)}, bf16[256,128]{1,0:T(8,128)(2,1)S(1)}, u32[]{:S(2)}, u32[]{:S(2)}) collective-permute-start(bf16[256,128]{1,0:T(8,128)(2,1)S(1)} %get-tuple-element.26), channel_id=1, source_target_pairs={{0,16},{8,24},{16,0},{24,8},{1,17},{9,25},{17,1},{25,9},{2,18},{10... | collective-permute-start | bytes 196616 | tf_op jit(solution)/shard_map/ppermute | solution.py:368
  11.6 4.7 %collective-permute-done.1.refs_2_ = bf16[256,128]{1,0:T(8,128)(2,1)S(1)} collective-permute-done((bf16[256,128]{1,0:T(8,128)(2,1)S(1)}, bf16[256,128]{1,0:T(8,128)(2,1)S(1)}, u32[]{:S(2)}, u32[]{:S(2)}) %collective-permute-start.1) | collective-permute-done | bytes 65568 | tf_op jit(solution)/shard_map/ppermute | solution.py:368
  16.3 1.4 %collective-permute-done.2.refs_3_ = bf16[256,128]{1,0:T(8,128)(2,1)S(1)} collective-permute-done((bf16[256,128]{1,0:T(8,128)(2,1)S(1)}, bf16[256,128]{1,0:T(8,128)(2,1)S(1)}, u32[]{:S(2)}, u32[]{:S(2)}) %collective-permute-start.2) | collective-permute-done | bytes 65568 | tf_op jit(solution)/shard_map/ppermute | solution.py:368
  18.1 1.6 %collective-permute-start.3 = (bf16[320,384]{1,0:T(8,128)(2,1)S(1)}, bf16[320,384]{1,0:T(8,128)(2,1)S(1)}, u32[]{:S(2)}, u32[]{:S(2)}) collective-permute-start(bf16[320,384]{1,0:T(8,128)(2,1)S(1)} %get-tuple-element.28.refs_0_.refs_4_), channel_id=1, source_target_pairs={{0,2},{2,0},{4,6},{6,4},{1,3},{3,1},{5,7},{7,5},{8,10},{10,8},{12,... | collective-permute-start | bytes 737288 | tf_op jit(solution)/shard_map/ppermute | solution.py:368
  19.7 1.5 %collective-permute-start.4 = (bf16[320,384]{1,0:T(8,128)(2,1)S(1)}, bf16[320,384]{1,0:T(8,128)(2,1)S(1)}, u32[]{:S(2)}, u32[]{:S(2)}) collective-permute-start(bf16[320,384]{1,0:T(8,128)(2,1)S(1)} %get-tuple-element.28.refs_0_.refs_4_), channel_id=1, source_target_pairs={{0,4},{2,6},{4,0},{6,2},{1,5},{3,7},{5,1},{7,3},{8,12},{10,14},{12... | collective-permute-start | bytes 737288 | tf_op jit(solution)/shard_map/ppermute | solution.py:368
  21.7 1.5 %collective-permute-start.10 = (bf16[320,384]{1,0:T(8,128)(2,1)S(1)}, bf16[320,384]{1,0:T(8,128)(2,1)S(1)}, u32[]{:S(2)}, u32[]{:S(2)}) collective-permute-start(bf16[320,384]{1,0:T(8,128)(2,1)S(1)} %get-tuple-element.39.refs_1_), channel_id=1, source_target_pairs={{0,4},{2,6},{4,0},{6,2},{1,5},{3,7},{5,1},{7,3},{8,12},{10,14},{12... | collective-permute-start | bytes 737288 | tf_op jit(solution)/shard_map/ppermute | solution.py:368
  23.2 1.4 %collective-permute-start.11 = (bf16[320,384]{1,0:T(8,128)(2,1)S(1)}, bf16[320,384]{1,0:T(8,128)(2,1)S(1)}, u32[]{:S(2)}, u32[]{:S(2)}) collective-permute-start(bf16[320,384]{1,0:T(8,128)(2,1)S(1)} %get-tuple-element.39.refs_1_), channel_id=1, source_target_pairs={{0,6},{2,4},{4,2},{6,0},{1,7},{3,5},{5,3},{7,1},{8,14},{10,12},{12... | collective-permute-start | bytes 737288 | tf_op jit(solution)/shard_map/ppermute | solution.py:368
  24.7 2.4 %collective-permute-done.3.refs_1_ = bf16[320,384]{1,0:T(8,128)(2,1)S(1)} collective-permute-done((bf16[320,384]{1,0:T(8,128)(2,1)S(1)}, bf16[320,384]{1,0:T(8,128)(2,1)S(1)}, u32[]{:S(2)}, u32[]{:S(2)}) %collective-permute-start.3) | collective-permute-done | bytes 245792 | tf_op jit(solution)/shard_map/ppermute | solution.py:368
  27.0 1.5 %collective-permute-start.9 = (bf16[320,384]{1,0:T(8,128)(2,1)S(1)}, bf16[320,384]{1,0:T(8,128)(2,1)S(1)}, u32[]{:S(2)}, u32[]{:S(2)}) collective-permute-start(bf16[320,384]{1,0:T(8,128)(2,1)S(1)} %get-tuple-element.39.refs_1_), channel_id=1, source_target_pairs={{0,2},{2,0},{4,6},{6,4},{1,3},{3,1},{5,7},{7,5},{8,10},{10,8},{12,... | collective-permute-start | bytes 737288 | tf_op jit(solution)/shard_map/ppermute | solution.py:368
  28.5 1.7 %copy-done = bf16[3,320,1280]{2,1,0:T(8,128)(2,1)S(1)} copy-done((bf16[3,320,1280]{2,1,0:T(8,128)(2,1)S(1)}, bf16[3,320,1280]{2,1,0:T(8,128)(2,1)}, u32[]{:S(2)}) %copy-start) | copy-done | bytes 2457624
  30.2 1.1 %copy-done.1 = bf16[320,1280]{1,0:T(8,128)(2,1)S(1)} copy-done((bf16[320,1280]{1,0:T(8,128)(2,1)S(1)}, bf16[320,1280]{1,0:T(8,128)(2,1)}, u32[]{:S(2)}) %copy-start.1) | copy-done | bytes 819224
  32.8 1.1 %shard_map.115 = (bf16[3,320,1280]{2,1,0:T(8,128)(2,1)S(1)}, bf16[1280,320]{1,0:T(8,128)(2,1)S(1)}, f32[2,1280,8]{2,1,0:T(8,128)S(1)}) custom-call(f32[10,128]{1,0:T(8,128)S(1)} %bitcast.6, f32[10,128]{1,0:T(8,128)S(1)} %bitcast.7, bf16[3,320,1280]{2,1,0:T(8,128)(2,1)S(1)} %copy-done, bf16[320,1280]{1,0:T(8,128)(2,1)S(1)} %copy-done.1), custom_call_target="tpu_custom_call" | custom-call | bytes 6291456 | tf_op jit(solution)/shard_map/pallas_call | solution.py:355
  33.9 4.8 %collective-permute-done.4.refs_2_ = bf16[320,384]{1,0:T(8,128)(2,1)S(1)} collective-permute-done((bf16[320,384]{1,0:T(8,128)(2,1)S(1)}, bf16[320,384]{1,0:T(8,128)(2,1)S(1)}, u32[]{:S(2)}, u32[]{:S(2)}) %collective-permute-start.4) | collective-permute-done | bytes 245792 | tf_op jit(solution)/shard_map/ppermute | solution.py:368
  38.7 4.1 %shard_map.116 = (bf16[320,384]{1,0:T(8,128)(2,1)S(1)}, bf16[320,384]{1,0:T(8,128)(2,1)S(1)}, bf16[320,384]{1,0:T(8,128)(2,1)S(1)}, bf16[320,384]{1,0:T(8,128)(2,1)S(1)}, bf16[320,384]{1,0:T(8,128)(2,1)S(1)}) custom-call(bf16[320,384]{1,0:T(8,128)(2,1)S(1)} %get-tuple-element.28.refs_0_.refs_4_, bf16[320,384]{1,0:T(8,128)(2,1)S(1)} %collective-permute-done.3.refs_1_, ...), custom_call_target="tpu_custom_call" | custom-call | bytes 12582912 | tf_op jit(solution)/shard_map/pallas_call | solution.py:355
  42.9 1.6 %shard_map.118 = (f32[4,400,128]{2,1,0:T(8,128)S(1)}, bf16[4,400,128]{2,1,0:T(8,128)(2,1)S(1)}) custom-call(bf16[320,384]{1,0:T(8,128)(2,1)S(1)} %get-tuple-element.38.refs_0_, bf16[320,384]{1,0:T(8,128)(2,1)S(1)} %get-tuple-element.39.refs_1_, bf16[320,384]{1,0:T(8,128)(2,1)S(1)} %collective-permute-done.9.refs_2_, ...), custom_call_target="tpu_custom_call" | custom-call | bytes 6291456 | tf_op jit(solution)/shard_map/pallas_call | solution.py:355
  44.6 2.0 %collective-permute-start.7 = (bf16[320,384]{1,0:T(8,128)(2,1)S(1)}, bf16[320,384]{1,0:T(8,128)(2,1)S(1)}, u32[]{:S(2)}, u32[]{:S(2)}) collective-permute-start(bf16[320,384]{1,0:T(8,128)(2,1)S(1)} %get-tuple-element.35), channel_id=1, source_target_pairs={{0,4},{2,6},{4,0},{6,2},{1,5},{3,7},{5,1},{7,3},{8,12},{10,14},{12... | collective-permute-start | bytes 737288 | tf_op jit(solution)/shard_map/ppermute | solution.py:368
  46.6 1.4 %collective-permute-start.8 = (bf16[320,384]{1,0:T(8,128)(2,1)S(1)}, bf16[320,384]{1,0:T(8,128)(2,1)S(1)}, u32[]{:S(2)}, u32[]{:S(2)}) collective-permute-start(bf16[320,384]{1,0:T(8,128)(2,1)S(1)} %get-tuple-element.36), channel_id=1, source_target_pairs={{0,6},{2,4},{4,2},{6,0},{1,7},{3,5},{5,3},{7,1},{8,14},{10,12},{12... | collective-permute-start | bytes 737288 | tf_op jit(solution)/shard_map/ppermute | solution.py:368
  48.5 1.8 %collective-permute-start.14 = (bf16[400,128]{1,0:T(8,128)(2,1)S(1)}, bf16[400,128]{1,0:T(8,128)(2,1)S(1)}, u32[]{:S(2)}, u32[]{:S(2)}) collective-permute-start(bf16[400,128]{1,0:T(8,128)(2,1)S(1)} %get-tuple-element.44), channel_id=1, source_target_pairs={{0,16},{8,24},{16,0},{24,8},{1,17},{9,25},{17,1},{25,9},{2,18},{10... | collective-permute-start | bytes 307208 | tf_op jit(solution)/shard_map/ppermute | solution.py:368
  50.3 3.1 %collective-permute-done.6.refs_1_ = bf16[320,384]{1,0:T(8,128)(2,1)S(1)} collective-permute-done((bf16[320,384]{1,0:T(8,128)(2,1)S(1)}, bf16[320,384]{1,0:T(8,128)(2,1)S(1)}, u32[]{:S(2)}, u32[]{:S(2)}) %collective-permute-start.6) | collective-permute-done | bytes 245792 | tf_op jit(solution)/shard_map/ppermute | solution.py:368
  54.5 3.0 %collective-permute-done.7.refs_2_ = bf16[320,384]{1,0:T(8,128)(2,1)S(1)} collective-permute-done((bf16[320,384]{1,0:T(8,128)(2,1)S(1)}, bf16[320,384]{1,0:T(8,128)(2,1)S(1)}, u32[]{:S(2)}, u32[]{:S(2)}) %collective-permute-start.7) | collective-permute-done | bytes 245792 | tf_op jit(solution)/shard_map/ppermute | solution.py:368
  57.5 1.1 %collective-permute-done.8.refs_3_ = bf16[320,384]{1,0:T(8,128)(2,1)S(1)} collective-permute-done((bf16[320,384]{1,0:T(8,128)(2,1)S(1)}, bf16[320,384]{1,0:T(8,128)(2,1)S(1)}, u32[]{:S(2)}, u32[]{:S(2)}) %collective-permute-start.8) | collective-permute-done | bytes 245792 | tf_op jit(solution)/shard_map/ppermute | solution.py:368
  58.6 1.4 %shard_map.117 = bf16[320,576]{1,0:T(8,128)(2,1)} custom-call(bf16[320,384]{1,0:T(8,128)(2,1)S(1)} %get-tuple-element.33.refs_0_, bf16[320,384]{1,0:T(8,128)(2,1)S(1)} %collective-permute-done.6.refs_1_, bf16[320,384]{1,0:T(8,128)(2,1)S(1)} %collective-permute-done.7.refs_2_, bf16[320,384]{1,0:T(8,128)(2,1)S(1)} %collective-permute-done.8.refs_3_, ...), custom_call_target="tpu_custom_call" | custom-call | bytes 4194304 | tf_op jit(solution)/shard_map/pallas_call | solution.py:355
  (36 shorter events, 8.6 us)
Async XLA Ops:
  0.6 1.0 %copy-start.2 = (bf16[320,576]{1,0:T(8,128)(2,1)S(1)}, bf16[320,576]{1,0:T(8,128)(2,1)}, u32[]{:S(2)}) copy-start(bf16[320,576]{1,0:T(8,128)(2,1)} %refs_4_.1) | copy-start | bytes 1105924
  1.6 0.9 %copy-start.4 = (bf16[320,384]{1,0:T(8,128)(2,1)S(1)}, bf16[320,384]{1,0:T(8,128)(2,1)}, u32[]{:S(2)}) copy-start(bf16[320,384]{1,0:T(8,128)(2,1)} %refs_3_.2) | copy-start | bytes 737284
  2.6 0.7 %copy-start.7 = (s32[48]{0:T(128)S(1)}, s32[48]{0:T(128)}, u32[]{:S(2)}) copy-start(s32[48]{0:T(128)} %param.12) | copy-start | bytes 580
  5.9 5.7 %collective-permute-start = (bf16[256,128]{1,0:T(8,128)(2,1)S(1)}, bf16[256,128]{1,0:T(8,128)(2,1)S(1)}, u32[]{:S(2)}, u32[]{:S(2)}) collective-permute-start(bf16[256,128]{1,0:T(8,128)(2,1)S(1)} %get-tuple-element.25), channel_id=1, source_target_pairs={{0,8},{8,0},{16,24},{24,16},{1,9},{9,1},{17,25},{25,17},{2,10},{10... | collective-permute-start | bytes 196616 | tf_op jit(solution)/shard_map/ppermute | solution.py:368
  9.0 7.3 %collective-permute-start.1 = (bf16[256,128]{1,0:T(8,128)(2,1)S(1)}, bf16[256,128]{1,0:T(8,128)(2,1)S(1)}, u32[]{:S(2)}, u32[]{:S(2)}) collective-permute-start(bf16[256,128]{1,0:T(8,128)(2,1)S(1)} %get-tuple-element.26), channel_id=1, source_target_pairs={{0,16},{8,24},{16,0},{24,8},{1,17},{9,25},{17,1},{25,9},{2,18},{10... | collective-permute-start | bytes 196616 | tf_op jit(solution)/shard_map/ppermute | solution.py:368
  11.6 6.1 %collective-permute-start.2 = (bf16[256,128]{1,0:T(8,128)(2,1)S(1)}, bf16[256,128]{1,0:T(8,128)(2,1)S(1)}, u32[]{:S(2)}, u32[]{:S(2)}) collective-permute-start(bf16[256,128]{1,0:T(8,128)(2,1)S(1)} %get-tuple-element.27), channel_id=1, source_target_pairs={{0,24},{8,16},{16,8},{24,0},{1,25},{9,17},{17,9},{25,1},{2,26},{10... | collective-permute-start | bytes 196616 | tf_op jit(solution)/shard_map/ppermute | solution.py:368
  18.1 8.9 %collective-permute-start.3 = (bf16[320,384]{1,0:T(8,128)(2,1)S(1)}, bf16[320,384]{1,0:T(8,128)(2,1)S(1)}, u32[]{:S(2)}, u32[]{:S(2)}) collective-permute-start(bf16[320,384]{1,0:T(8,128)(2,1)S(1)} %get-tuple-element.28.refs_0_.refs_4_), channel_id=1, source_target_pairs={{0,2},{2,0},{4,6},{6,4},{1,3},{3,1},{5,7},{7,5},{8,10},{10,8},{12,... | collective-permute-start | bytes 737288 | tf_op jit(solution)/shard_map/ppermute | solution.py:368
  19.7 19.0 %collective-permute-start.4 = (bf16[320,384]{1,0:T(8,128)(2,1)S(1)}, bf16[320,384]{1,0:T(8,128)(2,1)S(1)}, u32[]{:S(2)}, u32[]{:S(2)}) collective-permute-start(bf16[320,384]{1,0:T(8,128)(2,1)S(1)} %get-tuple-element.28.refs_0_.refs_4_), channel_id=1, source_target_pairs={{0,4},{2,6},{4,0},{6,2},{1,5},{3,7},{5,1},{7,3},{8,12},{10,14},{12... | collective-permute-start | bytes 737288 | tf_op jit(solution)/shard_map/ppermute | solution.py:368
  21.2 17.5 %collective-permute-start.5 = (bf16[320,384]{1,0:T(8,128)(2,1)S(1)}, bf16[320,384]{1,0:T(8,128)(2,1)S(1)}, u32[]{:S(2)}, u32[]{:S(2)}) collective-permute-start(bf16[320,384]{1,0:T(8,128)(2,1)S(1)} %get-tuple-element.28.refs_0_.refs_4_), channel_id=1, source_target_pairs={{0,6},{2,4},{4,2},{6,0},{1,7},{3,5},{5,3},{7,1},{8,14},{10,12},{12... | collective-permute-start | bytes 737288 | tf_op jit(solution)/shard_map/ppermute | solution.py:368
  21.7 21.1 %collective-permute-start.10 = (bf16[320,384]{1,0:T(8,128)(2,1)S(1)}, bf16[320,384]{1,0:T(8,128)(2,1)S(1)}, u32[]{:S(2)}, u32[]{:S(2)}) collective-permute-start(bf16[320,384]{1,0:T(8,128)(2,1)S(1)} %get-tuple-element.39.refs_1_), channel_id=1, source_target_pairs={{0,4},{2,6},{4,0},{6,2},{1,5},{3,7},{5,1},{7,3},{8,12},{10,14},{12... | collective-permute-start | bytes 737288 | tf_op jit(solution)/shard_map/ppermute | solution.py:368
  23.2 19.6 %collective-permute-start.11 = (bf16[320,384]{1,0:T(8,128)(2,1)S(1)}, bf16[320,384]{1,0:T(8,128)(2,1)S(1)}, u32[]{:S(2)}, u32[]{:S(2)}) collective-permute-start(bf16[320,384]{1,0:T(8,128)(2,1)S(1)} %get-tuple-element.39.refs_1_), channel_id=1, source_target_pairs={{0,6},{2,4},{4,2},{6,0},{1,7},{3,5},{5,3},{7,1},{8,14},{10,12},{12... | collective-permute-start | bytes 737288 | tf_op jit(solution)/shard_map/ppermute | solution.py:368
  27.0 15.8 %collective-permute-start.9 = (bf16[320,384]{1,0:T(8,128)(2,1)S(1)}, bf16[320,384]{1,0:T(8,128)(2,1)S(1)}, u32[]{:S(2)}, u32[]{:S(2)}) collective-permute-start(bf16[320,384]{1,0:T(8,128)(2,1)S(1)} %get-tuple-element.39.refs_1_), channel_id=1, source_target_pairs={{0,2},{2,0},{4,6},{6,4},{1,3},{3,1},{5,7},{7,5},{8,10},{10,8},{12,... | collective-permute-start | bytes 737288 | tf_op jit(solution)/shard_map/ppermute | solution.py:368
  28.5 1.7 %copy-start = (bf16[3,320,1280]{2,1,0:T(8,128)(2,1)S(1)}, bf16[3,320,1280]{2,1,0:T(8,128)(2,1)}, u32[]{:S(2)}) copy-start(bf16[3,320,1280]{2,1,0:T(8,128)(2,1)} %refs_2_.1) | copy-start | bytes 7372804
  30.2 1.1 %copy-start.1 = (bf16[320,1280]{1,0:T(8,128)(2,1)S(1)}, bf16[320,1280]{1,0:T(8,128)(2,1)}, u32[]{:S(2)}) copy-start(bf16[320,1280]{1,0:T(8,128)(2,1)} %refs_3_.3) | copy-start | bytes 2457604
  31.4 0.7 %copy-start.5 = (f32[1280]{0:T(1024)S(1)}, f32[1280]{0:T(1024)}, u32[]{:S(2)}) copy-start(f32[1280]{0:T(1024)} %param.16) | copy-start | bytes 15364
  32.1 0.7 %copy-start.6 = (f32[1280]{0:T(1024)S(1)}, f32[1280]{0:T(1024)}, u32[]{:S(2)}) copy-start(f32[1280]{0:T(1024)} %param.17) | copy-start | bytes 15364
  42.8 15.8 %copy-start.3 = (bf16[320,576]{1,0:T(8,128)(2,1)S(1)}, bf16[320,576]{1,0:T(8,128)(2,1)}, u32[]{:S(2)}) copy-start(bf16[320,576]{1,0:T(8,128)(2,1)} %refs_7_.1) | copy-start | bytes 1105924
  44.5 3.6 %collective-permute-start.12 = (bf16[4,400,128]{2,1,0:T(8,128)(2,1)S(1)}, bf16[4,400,128]{2,1,0:T(8,128)(2,1)S(1)}, u32[]{:S(2)}, u32[]{:S(2)}) collective-permute-start(bf16[4,400,128]{2,1,0:T(8,128)(2,1)S(1)} %get-tuple-element.41), channel_id=1, source_target_pairs={{0,1},{1,0},{2,3},{3,2},{4,5},{5,4},{6,7},{7,6},{8,9},{9,8},{10,11... | collective-permute-start | bytes 1228808 | tf_op jit(solution)/shard_map/ppermute | solution.py:368
  44.5 8.9 %collective-permute-start.6 = (bf16[320,384]{1,0:T(8,128)(2,1)S(1)}, bf16[320,384]{1,0:T(8,128)(2,1)S(1)}, u32[]{:S(2)}, u32[]{:S(2)}) collective-permute-start(bf16[320,384]{1,0:T(8,128)(2,1)S(1)} %get-tuple-element.34), channel_id=1, source_target_pairs={{0,2},{2,0},{4,6},{6,4},{1,3},{3,1},{5,7},{7,5},{8,10},{10,8},{12,... | collective-permute-start | bytes 737288 | tf_op jit(solution)/shard_map/ppermute | solution.py:368
  44.6 12.9 %collective-permute-start.7 = (bf16[320,384]{1,0:T(8,128)(2,1)S(1)}, bf16[320,384]{1,0:T(8,128)(2,1)S(1)}, u32[]{:S(2)}, u32[]{:S(2)}) collective-permute-start(bf16[320,384]{1,0:T(8,128)(2,1)S(1)} %get-tuple-element.35), channel_id=1, source_target_pairs={{0,4},{2,6},{4,0},{6,2},{1,5},{3,7},{5,1},{7,3},{8,12},{10,14},{12... | collective-permute-start | bytes 737288 | tf_op jit(solution)/shard_map/ppermute | solution.py:368
  46.6 12.0 %collective-permute-start.8 = (bf16[320,384]{1,0:T(8,128)(2,1)S(1)}, bf16[320,384]{1,0:T(8,128)(2,1)S(1)}, u32[]{:S(2)}, u32[]{:S(2)}) collective-permute-start(bf16[320,384]{1,0:T(8,128)(2,1)S(1)} %get-tuple-element.36), channel_id=1, source_target_pairs={{0,6},{2,4},{4,2},{6,0},{1,7},{3,5},{5,3},{7,1},{8,14},{10,12},{12... | collective-permute-start | bytes 737288 | tf_op jit(solution)/shard_map/ppermute | solution.py:368
  48.2 11.9 %collective-permute-start.13 = (bf16[400,128]{1,0:T(8,128)(2,1)S(1)}, bf16[400,128]{1,0:T(8,128)(2,1)S(1)}, u32[]{:S(2)}, u32[]{:S(2)}) collective-permute-start(bf16[400,128]{1,0:T(8,128)(2,1)S(1)} %get-tuple-element.43), channel_id=1, source_target_pairs={{0,8},{8,0},{16,24},{24,16},{1,9},{9,1},{17,25},{25,17},{2,10},{10... | collective-permute-start | bytes 307208 | tf_op jit(solution)/shard_map/ppermute | solution.py:368
  48.5 11.5 %collective-permute-start.14 = (bf16[400,128]{1,0:T(8,128)(2,1)S(1)}, bf16[400,128]{1,0:T(8,128)(2,1)S(1)}, u32[]{:S(2)}, u32[]{:S(2)}) collective-permute-start(bf16[400,128]{1,0:T(8,128)(2,1)S(1)} %get-tuple-element.44), channel_id=1, source_target_pairs={{0,16},{8,24},{16,0},{24,8},{1,17},{9,25},{17,1},{25,9},{2,18},{10... | collective-permute-start | bytes 307208 | tf_op jit(solution)/shard_map/ppermute | solution.py:368
  53.4 6.6 %collective-permute-start.15 = (bf16[400,128]{1,0:T(8,128)(2,1)S(1)}, bf16[400,128]{1,0:T(8,128)(2,1)S(1)}, u32[]{:S(2)}, u32[]{:S(2)}) collective-permute-start(bf16[400,128]{1,0:T(8,128)(2,1)S(1)} %get-tuple-element.45), channel_id=1, source_target_pairs={{0,24},{8,16},{16,8},{24,0},{1,25},{9,17},{17,9},{25,1},{2,26},{10... | collective-permute-start | bytes 307208 | tf_op jit(solution)/shard_map/ppermute | solution.py:368
  (2 other events, 1.3 us)
where the time goes:
time: 61.2 us; the launch traced here: 60.8 us
  waiting for transfers between devices  20.6 us (34%)
  starting transfers between devices  20.5 us (33%)
  Pallas kernels  10.9 us (18%)
  local copies, waits for them, and re-layouts  8.14 us (13%)
  between operations  0.75 us (1%)
    ppermute x16, waiting for transfers between devices, swap(): lax.ppermute(value, axis, [(index, index ^ step) for index in range(count)])  20.6 us
    ppermute x16, starting transfers between devices, swap(): lax.ppermute(value, axis, [(index, index ^ step) for index in range(count)])  20.5 us
    pallas_call x8, Pallas kernels, call(): pl.pallas_call(kernel, out_shape=[jax.ShapeDtypeStruct(shape, kind) for s...  10.9 us
    unnamed x20, local copies, waits for them, and re-layouts  8.14 us
  transfers between devices with their start and end apart: 16, of which 7 were waited for; matrix products, arithmetic and copies ran while one was open for 0% of the time, Pallas kernels for 11%

commit v1 on v0

--- a/solution.py
+++ b/solution.py
@@ -168,8 +168,19 @@
     return mm(wide, picker)[0:1]
 
 
-def pack_kernel(plan, slot_ref, length_ref, start_ref, patches_ref, cot_ref, *refs):
+def pack_kernel(plan, slot_hbm, length_hbm, start_hbm, patches_hbm, cot_hbm, *refs):
     outs, cot_out, pos_out, rows = refs[: plan.dp], refs[plan.dp], refs[plan.dp + 1], refs[plan.dp + 2]
+    slot_ref, length_ref, start_ref, patches_ref, cot_ref, done = refs[plan.dp + 3 :]
+    held = (slot_ref, length_ref, start_ref, patches_ref, cot_ref)
+    given = (slot_hbm, length_hbm, start_hbm, patches_hbm, cot_hbm)
+    copies = [
+        pltpu.make_async_copy(source, target, done.at[index])
+        for index, (source, target) in enumerate(zip(given, held))
+    ]
+    for copy in copies:
+        copy.start()
+    for copy in copies[:4]:
+        copy.wait()
     mine = lax.axis_index("dp")
     flat, shift, block = plan.flat, plan.shift, plan.block
     lane = iota((1, flat), 1)
@@ -201,6 +212,7 @@
     position = (high * 16.0 + low).astype(jnp.int32) + inner
     pos_out[...] = jnp.broadcast_to(position, (8, flat))
     chosen = onehot(iota((plan.seq, flat), 0) == position)
+    copies[4].wait()
     cot_out[...] = mm(cot_ref[...], chosen).astype(jnp.bfloat16)
 
 
@@ -346,6 +358,11 @@
 
 
 VMEM = pl.BlockSpec(memory_space=pltpu.VMEM)
+FAR = pl.BlockSpec(memory_space=pltpu.HBM)
+
+
+def far(value):
+    return pltpu.with_memory_space_constraint(value, pltpu.HBM)
 
 
 def call(body, plan, outs, scratch, *operands, space, cost, specs=None):
@@ -377,9 +394,15 @@
     packed = call(
         pack_kernel, plan,
         [((height, LANES), half)] * plan.dp + [((cols, flat), half), ((8, flat), jnp.int32)],
-        [pltpu.VMEM((height, flat), half)],
-        slot_plan[None], lengths[None], starts[None], patches, cotangent,
-        space=8, cost=3,
+        [
+            pltpu.VMEM((height, flat), half),
+            *[pltpu.VMEM((1, count), jnp.int32) for count in (plan.images, plan.images, plan.slots)],
+            pltpu.VMEM(patches.shape, half),
+            pltpu.VMEM(cotangent.shape, half),
+            pltpu.SemaphoreType.DMA((5,)),
+        ],
+        *[far(value) for value in (slot_plan[None], lengths[None], starts[None], patches, cotangent)],
+        space=8, cost=3, specs=[FAR] * 5,
     )
     blocks, own_cot, positions = packed[: plan.dp], packed[plan.dp], packed[plan.dp + 1]
     arrived = [blocks[0]] + [swap(blocks[step], "dp", step) for step in range(1, plan.dp)]
@@ -395,9 +418,8 @@
         prepare_kernel, plan,
         [(w_qkv.shape, half), ((width, cols), half), ((2, width, 8), single)],
         [pltpu.SemaphoreType.DMA],
-        ln_gain.reshape(-1, LANES), ln_bias.reshape(-1, LANES), w_qkv, w_out,
-        space=10, cost=6,
-        specs=[VMEM, VMEM, pl.BlockSpec(memory_space=pltpu.HBM), VMEM],
+        ln_gain.reshape(-1, LANES), ln_bias.reshape(-1, LANES), far(w_qkv), w_out,
+        space=10, cost=6, specs=[VMEM, VMEM, FAR, VMEM],
     )
     attended = call(
         attend_kernel, plan,

time: 61.2 us -> 58.4 us (0.954)
  local copies, waits for them, and re-layouts: 8.14 us -> 2.54 us
  Pallas kernels: 10.9 us -> 12.6 us
  waiting for transfers between devices: 20.6 us -> 21.7 us
    unnamed x20 -> x8, local copies, waits for them, and re-layouts: 8.14 us -> 2.54 us
    pallas_call x8, Pallas kernels: 10.9 us -> 12.6 us  [call(): pl.pallas_call(kernel, out_shape=[jax.ShapeDtypeStruct(shape, kind) for s...]
    ppermute x16, waiting for transfers between devices: 20.6 us -> 21.7 us  [swap(): lax.ppermute(value, axis, [(index, index ^ step) for index in range(count)])]
  transfers between devices with their start and end apart: 16 -> 16, of which waited for: 7 -> 7; matrix products, arithmetic and copies ran while one was open for 0% -> 0% of each run, Pallas kernels for 11% -> 13%
where the time goes in v1:
time: 58.4 us; the launch traced here: 58.1 us
  waiting for transfers between devices  21.7 us (37%)
  starting transfers between devices  20.4 us (35%)
  Pallas kernels  12.6 us (22%)
  local copies, waits for them, and re-layouts  2.54 us (4%)
  between operations  0.74 us (1%)
    ppermute x16, waiting for transfers between devices, swap(): lax.ppermute(value, axis, [(index, index ^ step) for index in range(count)])  21.7 us
    ppermute x16, starting transfers between devices, swap(): lax.ppermute(value, axis, [(index, index ^ step) for index in range(count)])  20.4 us
    pallas_call x8, Pallas kernels, call(): pl.pallas_call(kernel, out_shape=[jax.ShapeDtypeStruct(shape, kind) for s...  12.6 us
    unnamed x8, local copies, waits for them, and re-layouts  2.54 us
  transfers between devices with their start and end apart: 16, of which 7 were waited for; matrix products, arithmetic and copies ran while one was open for 0% of the time, Pallas kernels for 13%

profile of v1, /device:TPU:0, one launch (start us, length us, event | category | flops | bytes accessed | tf_op | source)
XLA Modules:
  0.0 58.1 jit_solution(11491742996644646111)
XLA Ops:
  0.6 2.5 %shard_map.113 = (bf16[256,128]{1,0:T(8,128)(2,1)S(1)}, bf16[256,128]{1,0:T(8,128)(2,1)S(1)}, bf16[256,128]{1,0:T(8,128)(2,1)S(1)}, bf16[256,128]{1,0:T(8,128)(2...) custom-call(s32[1,48]{1,0:T(1,128)} %bitcast.9, s32[1,48]{1,0:T(1,128)} %bitcast.10, s32[1,48]{1,0:T(1,128)} %bitcast.11, ...), custom_call_target="tpu_custom_call" | custom-call | bytes 3145728 | tf_op jit(solution)/shard_map/pallas_call | solution.py:372
  3.1 3.1 %collective-permute-start = (bf16[256,128]{1,0:T(8,128)(2,1)S(1)}, bf16[256,128]{1,0:T(8,128)(2,1)S(1)}, u32[]{:S(2)}, u32[]{:S(2)}) collective-permute-start(bf16[256,128]{1,0:T(8,128)(2,1)S(1)} %get-tuple-element.25), channel_id=1, source_target_pairs={{0,8},{8,0},{16,24},{24,16},{1,9},{9,1},{17,25},{25,17},{2,10},{10... | collective-permute-start | bytes 196616 | tf_op jit(solution)/shard_map/ppermute | solution.py:385
  6.2 2.6 %collective-permute-start.1 = (bf16[256,128]{1,0:T(8,128)(2,1)S(1)}, bf16[256,128]{1,0:T(8,128)(2,1)S(1)}, u32[]{:S(2)}, u32[]{:S(2)}) collective-permute-start(bf16[256,128]{1,0:T(8,128)(2,1)S(1)} %get-tuple-element.26), channel_id=1, source_target_pairs={{0,16},{8,24},{16,0},{24,8},{1,17},{9,25},{17,1},{25,9},{2,18},{10... | collective-permute-start | bytes 196616 | tf_op jit(solution)/shard_map/ppermute | solution.py:385
  8.8 4.7 %collective-permute-done.1.refs_2_ = bf16[256,128]{1,0:T(8,128)(2,1)S(1)} collective-permute-done((bf16[256,128]{1,0:T(8,128)(2,1)S(1)}, bf16[256,128]{1,0:T(8,128)(2,1)S(1)}, u32[]{:S(2)}, u32[]{:S(2)}) %collective-permute-start.1) | collective-permute-done | bytes 65568 | tf_op jit(solution)/shard_map/ppermute | solution.py:385
  13.5 1.4 %collective-permute-done.2.refs_3_ = bf16[256,128]{1,0:T(8,128)(2,1)S(1)} collective-permute-done((bf16[256,128]{1,0:T(8,128)(2,1)S(1)}, bf16[256,128]{1,0:T(8,128)(2,1)S(1)}, u32[]{:S(2)}, u32[]{:S(2)}) %collective-permute-start.2) | collective-permute-done | bytes 65568 | tf_op jit(solution)/shard_map/ppermute | solution.py:385
  15.4 1.5 %collective-permute-start.3 = (bf16[320,384]{1,0:T(8,128)(2,1)S(1)}, bf16[320,384]{1,0:T(8,128)(2,1)S(1)}, u32[]{:S(2)}, u32[]{:S(2)}) collective-permute-start(bf16[320,384]{1,0:T(8,128)(2,1)S(1)} %get-tuple-element.28.refs_0_.refs_4_), channel_id=1, source_target_pairs={{0,2},{2,0},{4,6},{6,4},{1,3},{3,1},{5,7},{7,5},{8,10},{10,8},{12,... | collective-permute-start | bytes 737288 | tf_op jit(solution)/shard_map/ppermute | solution.py:385
  16.9 1.5 %collective-permute-start.4 = (bf16[320,384]{1,0:T(8,128)(2,1)S(1)}, bf16[320,384]{1,0:T(8,128)(2,1)S(1)}, u32[]{:S(2)}, u32[]{:S(2)}) collective-permute-start(bf16[320,384]{1,0:T(8,128)(2,1)S(1)} %get-tuple-element.28.refs_0_.refs_4_), channel_id=1, source_target_pairs={{0,4},{2,6},{4,0},{6,2},{1,5},{3,7},{5,1},{7,3},{8,12},{10,14},{12... | collective-permute-start | bytes 737288 | tf_op jit(solution)/shard_map/ppermute | solution.py:385
  19.0 1.5 %collective-permute-start.10 = (bf16[320,384]{1,0:T(8,128)(2,1)S(1)}, bf16[320,384]{1,0:T(8,128)(2,1)S(1)}, u32[]{:S(2)}, u32[]{:S(2)}) collective-permute-start(bf16[320,384]{1,0:T(8,128)(2,1)S(1)} %get-tuple-element.39.refs_1_), channel_id=1, source_target_pairs={{0,4},{2,6},{4,0},{6,2},{1,5},{3,7},{5,1},{7,3},{8,12},{10,14},{12... | collective-permute-start | bytes 737288 | tf_op jit(solution)/shard_map/ppermute | solution.py:385
  20.5 1.4 %collective-permute-start.11 = (bf16[320,384]{1,0:T(8,128)(2,1)S(1)}, bf16[320,384]{1,0:T(8,128)(2,1)S(1)}, u32[]{:S(2)}, u32[]{:S(2)}) collective-permute-start(bf16[320,384]{1,0:T(8,128)(2,1)S(1)} %get-tuple-element.39.refs_1_), channel_id=1, source_target_pairs={{0,6},{2,4},{4,2},{6,0},{1,7},{3,5},{5,3},{7,1},{8,14},{10,12},{12... | collective-permute-start | bytes 737288 | tf_op jit(solution)/shard_map/ppermute | solution.py:385
  21.9 2.4 %collective-permute-done.3.refs_1_ = bf16[320,384]{1,0:T(8,128)(2,1)S(1)} collective-permute-done((bf16[320,384]{1,0:T(8,128)(2,1)S(1)}, bf16[320,384]{1,0:T(8,128)(2,1)S(1)}, u32[]{:S(2)}, u32[]{:S(2)}) %collective-permute-start.3) | collective-permute-done | bytes 245792 | tf_op jit(solution)/shard_map/ppermute | solution.py:385
  24.3 1.5 %collective-permute-start.9 = (bf16[320,384]{1,0:T(8,128)(2,1)S(1)}, bf16[320,384]{1,0:T(8,128)(2,1)S(1)}, u32[]{:S(2)}, u32[]{:S(2)}) collective-permute-start(bf16[320,384]{1,0:T(8,128)(2,1)S(1)} %get-tuple-element.39.refs_1_), channel_id=1, source_target_pairs={{0,2},{2,0},{4,6},{6,4},{1,3},{3,1},{5,7},{7,5},{8,10},{10,8},{12,... | collective-permute-start | bytes 737288 | tf_op jit(solution)/shard_map/ppermute | solution.py:385
  25.8 1.1 %copy-done = bf16[320,1280]{1,0:T(8,128)(2,1)S(1)} copy-done((bf16[320,1280]{1,0:T(8,128)(2,1)S(1)}, bf16[320,1280]{1,0:T(8,128)(2,1)}, u32[]{:S(2)}) %copy-start) | copy-done | bytes 819224
  28.3 1.7 %shard_map.115 = (bf16[3,320,1280]{2,1,0:T(8,128)(2,1)S(1)}, bf16[1280,320]{1,0:T(8,128)(2,1)S(1)}, f32[2,1280,8]{2,1,0:T(8,128)S(1)}) custom-call(f32[10,128]{1,0:T(8,128)S(1)} %bitcast.6, f32[10,128]{1,0:T(8,128)S(1)} %bitcast.7, bf16[3,320,1280]{2,1,0:T(8,128)(2,1)} %refs_2_.1, bf16[320,1280]{1,0:T(8,128)(2,1)S(1)} %copy-done), custom_call_target="tpu_custom_call" | custom-call | bytes 6291456 | tf_op jit(solution)/shard_map/pallas_call | solution.py:372
  30.0 5.9 %collective-permute-done.4.refs_2_ = bf16[320,384]{1,0:T(8,128)(2,1)S(1)} collective-permute-done((bf16[320,384]{1,0:T(8,128)(2,1)S(1)}, bf16[320,384]{1,0:T(8,128)(2,1)S(1)}, u32[]{:S(2)}, u32[]{:S(2)}) %collective-permute-start.4) | collective-permute-done | bytes 245792 | tf_op jit(solution)/shard_map/ppermute | solution.py:385
  35.9 4.1 %shard_map.116 = (bf16[320,384]{1,0:T(8,128)(2,1)S(1)}, bf16[320,384]{1,0:T(8,128)(2,1)S(1)}, bf16[320,384]{1,0:T(8,128)(2,1)S(1)}, bf16[320,384]{1,0:T(8,128)(2,1)S(1)}, bf16[320,384]{1,0:T(8,128)(2,1)S(1)}) custom-call(bf16[320,384]{1,0:T(8,128)(2,1)S(1)} %get-tuple-element.28.refs_0_.refs_4_, bf16[320,384]{1,0:T(8,128)(2,1)S(1)} %collective-permute-done.3.refs_1_, ...), custom_call_target="tpu_custom_call" | custom-call | bytes 12582912 | tf_op jit(solution)/shard_map/pallas_call | solution.py:372
  40.1 1.6 %shard_map.118 = (f32[4,400,128]{2,1,0:T(8,128)S(1)}, bf16[4,400,128]{2,1,0:T(8,128)(2,1)S(1)}) custom-call(bf16[320,384]{1,0:T(8,128)(2,1)S(1)} %get-tuple-element.38.refs_0_, bf16[320,384]{1,0:T(8,128)(2,1)S(1)} %get-tuple-element.39.refs_1_, bf16[320,384]{1,0:T(8,128)(2,1)S(1)} %collective-permute-done.9.refs_2_, ...), custom_call_target="tpu_custom_call" | custom-call | bytes 6291456 | tf_op jit(solution)/shard_map/pallas_call | solution.py:372
  41.8 2.0 %collective-permute-start.7 = (bf16[320,384]{1,0:T(8,128)(2,1)S(1)}, bf16[320,384]{1,0:T(8,128)(2,1)S(1)}, u32[]{:S(2)}, u32[]{:S(2)}) collective-permute-start(bf16[320,384]{1,0:T(8,128)(2,1)S(1)} %get-tuple-element.35), channel_id=1, source_target_pairs={{0,4},{2,6},{4,0},{6,2},{1,5},{3,7},{5,1},{7,3},{8,12},{10,14},{12... | collective-permute-start | bytes 737288 | tf_op jit(solution)/shard_map/ppermute | solution.py:385
  43.9 1.5 %collective-permute-start.8 = (bf16[320,384]{1,0:T(8,128)(2,1)S(1)}, bf16[320,384]{1,0:T(8,128)(2,1)S(1)}, u32[]{:S(2)}, u32[]{:S(2)}) collective-permute-start(bf16[320,384]{1,0:T(8,128)(2,1)S(1)} %get-tuple-element.36), channel_id=1, source_target_pairs={{0,6},{2,4},{4,2},{6,0},{1,7},{3,5},{5,3},{7,1},{8,14},{10,12},{12... | collective-permute-start | bytes 737288 | tf_op jit(solution)/shard_map/ppermute | solution.py:385
  45.7 1.8 %collective-permute-start.14 = (bf16[400,128]{1,0:T(8,128)(2,1)S(1)}, bf16[400,128]{1,0:T(8,128)(2,1)S(1)}, u32[]{:S(2)}, u32[]{:S(2)}) collective-permute-start(bf16[400,128]{1,0:T(8,128)(2,1)S(1)} %get-tuple-element.44), channel_id=1, source_target_pairs={{0,16},{8,24},{16,0},{24,8},{1,17},{9,25},{17,1},{25,9},{2,18},{10... | collective-permute-start | bytes 307208 | tf_op jit(solution)/shard_map/ppermute | solution.py:385
  47.5 3.1 %collective-permute-done.6.refs_1_ = bf16[320,384]{1,0:T(8,128)(2,1)S(1)} collective-permute-done((bf16[320,384]{1,0:T(8,128)(2,1)S(1)}, bf16[320,384]{1,0:T(8,128)(2,1)S(1)}, u32[]{:S(2)}, u32[]{:S(2)}) %collective-permute-start.6) | collective-permute-done | bytes 245792 | tf_op jit(solution)/shard_map/ppermute | solution.py:385
  50.7 1.0 %collective-permute-start.15 = (bf16[400,128]{1,0:T(8,128)(2,1)S(1)}, bf16[400,128]{1,0:T(8,128)(2,1)S(1)}, u32[]{:S(2)}, u32[]{:S(2)}) collective-permute-start(bf16[400,128]{1,0:T(8,128)(2,1)S(1)} %get-tuple-element.45), channel_id=1, source_target_pairs={{0,24},{8,16},{16,8},{24,0},{1,25},{9,17},{17,9},{25,1},{2,26},{10... | collective-permute-start | bytes 307208 | tf_op jit(solution)/shard_map/ppermute | solution.py:385
  51.7 3.0 %collective-permute-done.7.refs_2_ = bf16[320,384]{1,0:T(8,128)(2,1)S(1)} collective-permute-done((bf16[320,384]{1,0:T(8,128)(2,1)S(1)}, bf16[320,384]{1,0:T(8,128)(2,1)S(1)}, u32[]{:S(2)}, u32[]{:S(2)}) %collective-permute-start.7) | collective-permute-done | bytes 245792 | tf_op jit(solution)/shard_map/ppermute | solution.py:385
  54.7 1.2 %collective-permute-done.8.refs_3_ = bf16[320,384]{1,0:T(8,128)(2,1)S(1)} collective-permute-done((bf16[320,384]{1,0:T(8,128)(2,1)S(1)}, bf16[320,384]{1,0:T(8,128)(2,1)S(1)}, u32[]{:S(2)}, u32[]{:S(2)}) %collective-permute-start.8) | collective-permute-done | bytes 245792 | tf_op jit(solution)/shard_map/ppermute | solution.py:385
  55.9 1.4 %shard_map.117 = bf16[320,576]{1,0:T(8,128)(2,1)} custom-call(bf16[320,384]{1,0:T(8,128)(2,1)S(1)} %get-tuple-element.33.refs_0_, bf16[320,384]{1,0:T(8,128)(2,1)S(1)} %collective-permute-done.6.refs_1_, bf16[320,384]{1,0:T(8,128)(2,1)S(1)} %collective-permute-done.7.refs_2_, bf16[320,384]{1,0:T(8,128)(2,1)S(1)} %collective-permute-done.8.refs_3_, ...), custom_call_target="tpu_custom_call" | custom-call | bytes 4194304 | tf_op jit(solution)/shard_map/pallas_call | solution.py:372
  (24 shorter events, 3.8 us)
Async XLA Ops:
  3.1 5.7 %collective-permute-start = (bf16[256,128]{1,0:T(8,128)(2,1)S(1)}, bf16[256,128]{1,0:T(8,128)(2,1)S(1)}, u32[]{:S(2)}, u32[]{:S(2)}) collective-permute-start(bf16[256,128]{1,0:T(8,128)(2,1)S(1)} %get-tuple-element.25), channel_id=1, source_target_pairs={{0,8},{8,0},{16,24},{24,16},{1,9},{9,1},{17,25},{25,17},{2,10},{10... | collective-permute-start | bytes 196616 | tf_op jit(solution)/shard_map/ppermute | solution.py:385
  6.2 7.3 %collective-permute-start.1 = (bf16[256,128]{1,0:T(8,128)(2,1)S(1)}, bf16[256,128]{1,0:T(8,128)(2,1)S(1)}, u32[]{:S(2)}, u32[]{:S(2)}) collective-permute-start(bf16[256,128]{1,0:T(8,128)(2,1)S(1)} %get-tuple-element.26), channel_id=1, source_target_pairs={{0,16},{8,24},{16,0},{24,8},{1,17},{9,25},{17,1},{25,9},{2,18},{10... | collective-permute-start | bytes 196616 | tf_op jit(solution)/shard_map/ppermute | solution.py:385
  8.8 6.1 %collective-permute-start.2 = (bf16[256,128]{1,0:T(8,128)(2,1)S(1)}, bf16[256,128]{1,0:T(8,128)(2,1)S(1)}, u32[]{:S(2)}, u32[]{:S(2)}) collective-permute-start(bf16[256,128]{1,0:T(8,128)(2,1)S(1)} %get-tuple-element.27), channel_id=1, source_target_pairs={{0,24},{8,16},{16,8},{24,0},{1,25},{9,17},{17,9},{25,1},{2,26},{10... | collective-permute-start | bytes 196616 | tf_op jit(solution)/shard_map/ppermute | solution.py:385
  15.4 8.9 %collective-permute-start.3 = (bf16[320,384]{1,0:T(8,128)(2,1)S(1)}, bf16[320,384]{1,0:T(8,128)(2,1)S(1)}, u32[]{:S(2)}, u32[]{:S(2)}) collective-permute-start(bf16[320,384]{1,0:T(8,128)(2,1)S(1)} %get-tuple-element.28.refs_0_.refs_4_), channel_id=1, source_target_pairs={{0,2},{2,0},{4,6},{6,4},{1,3},{3,1},{5,7},{7,5},{8,10},{10,8},{12,... | collective-permute-start | bytes 737288 | tf_op jit(solution)/shard_map/ppermute | solution.py:385
  16.9 18.9 %collective-permute-start.4 = (bf16[320,384]{1,0:T(8,128)(2,1)S(1)}, bf16[320,384]{1,0:T(8,128)(2,1)S(1)}, u32[]{:S(2)}, u32[]{:S(2)}) collective-permute-start(bf16[320,384]{1,0:T(8,128)(2,1)S(1)} %get-tuple-element.28.refs_0_.refs_4_), channel_id=1, source_target_pairs={{0,4},{2,6},{4,0},{6,2},{1,5},{3,7},{5,1},{7,3},{8,12},{10,14},{12... | collective-permute-start | bytes 737288 | tf_op jit(solution)/shard_map/ppermute | solution.py:385
  18.5 17.4 %collective-permute-start.5 = (bf16[320,384]{1,0:T(8,128)(2,1)S(1)}, bf16[320,384]{1,0:T(8,128)(2,1)S(1)}, u32[]{:S(2)}, u32[]{:S(2)}) collective-permute-start(bf16[320,384]{1,0:T(8,128)(2,1)S(1)} %get-tuple-element.28.refs_0_.refs_4_), channel_id=1, source_target_pairs={{0,6},{2,4},{4,2},{6,0},{1,7},{3,5},{5,3},{7,1},{8,14},{10,12},{12... | collective-permute-start | bytes 737288 | tf_op jit(solution)/shard_map/ppermute | solution.py:385
  19.0 21.1 %collective-permute-start.10 = (bf16[320,384]{1,0:T(8,128)(2,1)S(1)}, bf16[320,384]{1,0:T(8,128)(2,1)S(1)}, u32[]{:S(2)}, u32[]{:S(2)}) collective-permute-start(bf16[320,384]{1,0:T(8,128)(2,1)S(1)} %get-tuple-element.39.refs_1_), channel_id=1, source_target_pairs={{0,4},{2,6},{4,0},{6,2},{1,5},{3,7},{5,1},{7,3},{8,12},{10,14},{12... | collective-permute-start | bytes 737288 | tf_op jit(solution)/shard_map/ppermute | solution.py:385
  20.5 19.6 %collective-permute-start.11 = (bf16[320,384]{1,0:T(8,128)(2,1)S(1)}, bf16[320,384]{1,0:T(8,128)(2,1)S(1)}, u32[]{:S(2)}, u32[]{:S(2)}) collective-permute-start(bf16[320,384]{1,0:T(8,128)(2,1)S(1)} %get-tuple-element.39.refs_1_), channel_id=1, source_target_pairs={{0,6},{2,4},{4,2},{6,0},{1,7},{3,5},{5,3},{7,1},{8,14},{10,12},{12... | collective-permute-start | bytes 737288 | tf_op jit(solution)/shard_map/ppermute | solution.py:385
  24.3 15.8 %collective-permute-start.9 = (bf16[320,384]{1,0:T(8,128)(2,1)S(1)}, bf16[320,384]{1,0:T(8,128)(2,1)S(1)}, u32[]{:S(2)}, u32[]{:S(2)}) collective-permute-start(bf16[320,384]{1,0:T(8,128)(2,1)S(1)} %get-tuple-element.39.refs_1_), channel_id=1, source_target_pairs={{0,2},{2,0},{4,6},{6,4},{1,3},{3,1},{5,7},{7,5},{8,10},{10,8},{12,... | collective-permute-start | bytes 737288 | tf_op jit(solution)/shard_map/ppermute | solution.py:385
  25.8 1.1 %copy-start = (bf16[320,1280]{1,0:T(8,128)(2,1)S(1)}, bf16[320,1280]{1,0:T(8,128)(2,1)}, u32[]{:S(2)}) copy-start(bf16[320,1280]{1,0:T(8,128)(2,1)} %refs_3_.3) | copy-start | bytes 2457604
  26.9 0.7 %copy-start.2 = (f32[1280]{0:T(1024)S(1)}, f32[1280]{0:T(1024)}, u32[]{:S(2)}) copy-start(f32[1280]{0:T(1024)} %param.16) | copy-start | bytes 15364
  27.6 0.7 %copy-start.3 = (f32[1280]{0:T(1024)S(1)}, f32[1280]{0:T(1024)}, u32[]{:S(2)}) copy-start(f32[1280]{0:T(1024)} %param.17) | copy-start | bytes 15364
  40.0 15.8 %copy-start.1 = (bf16[320,576]{1,0:T(8,128)(2,1)S(1)}, bf16[320,576]{1,0:T(8,128)(2,1)}, u32[]{:S(2)}) copy-start(bf16[320,576]{1,0:T(8,128)(2,1)} %refs_7_.1) | copy-start | bytes 1105924
  41.7 3.6 %collective-permute-start.12 = (bf16[4,400,128]{2,1,0:T(8,128)(2,1)S(1)}, bf16[4,400,128]{2,1,0:T(8,128)(2,1)S(1)}, u32[]{:S(2)}, u32[]{:S(2)}) collective-permute-start(bf16[4,400,128]{2,1,0:T(8,128)(2,1)S(1)} %get-tuple-element.41), channel_id=1, source_target_pairs={{0,1},{1,0},{2,3},{3,2},{4,5},{5,4},{6,7},{7,6},{8,9},{9,8},{10,11... | collective-permute-start | bytes 1228808 | tf_op jit(solution)/shard_map/ppermute | solution.py:385
  41.8 8.9 %collective-permute-start.6 = (bf16[320,384]{1,0:T(8,128)(2,1)S(1)}, bf16[320,384]{1,0:T(8,128)(2,1)S(1)}, u32[]{:S(2)}, u32[]{:S(2)}) collective-permute-start(bf16[320,384]{1,0:T(8,128)(2,1)S(1)} %get-tuple-element.34), channel_id=1, source_target_pairs={{0,2},{2,0},{4,6},{6,4},{1,3},{3,1},{5,7},{7,5},{8,10},{10,8},{12,... | collective-permute-start | bytes 737288 | tf_op jit(solution)/shard_map/ppermute | solution.py:385
  41.8 12.8 %collective-permute-start.7 = (bf16[320,384]{1,0:T(8,128)(2,1)S(1)}, bf16[320,384]{1,0:T(8,128)(2,1)S(1)}, u32[]{:S(2)}, u32[]{:S(2)}) collective-permute-start(bf16[320,384]{1,0:T(8,128)(2,1)S(1)} %get-tuple-element.35), channel_id=1, source_target_pairs={{0,4},{2,6},{4,0},{6,2},{1,5},{3,7},{5,1},{7,3},{8,12},{10,14},{12... | collective-permute-start | bytes 737288 | tf_op jit(solution)/shard_map/ppermute | solution.py:385
  43.9 12.0 %collective-permute-start.8 = (bf16[320,384]{1,0:T(8,128)(2,1)S(1)}, bf16[320,384]{1,0:T(8,128)(2,1)S(1)}, u32[]{:S(2)}, u32[]{:S(2)}) collective-permute-start(bf16[320,384]{1,0:T(8,128)(2,1)S(1)} %get-tuple-element.36), channel_id=1, source_target_pairs={{0,6},{2,4},{4,2},{6,0},{1,7},{3,5},{5,3},{7,1},{8,14},{10,12},{12... | collective-permute-start | bytes 737288 | tf_op jit(solution)/shard_map/ppermute | solution.py:385
  45.4 11.9 %collective-permute-start.13 = (bf16[400,128]{1,0:T(8,128)(2,1)S(1)}, bf16[400,128]{1,0:T(8,128)(2,1)S(1)}, u32[]{:S(2)}, u32[]{:S(2)}) collective-permute-start(bf16[400,128]{1,0:T(8,128)(2,1)S(1)} %get-tuple-element.43), channel_id=1, source_target_pairs={{0,8},{8,0},{16,24},{24,16},{1,9},{9,1},{17,25},{25,17},{2,10},{10... | collective-permute-start | bytes 307208 | tf_op jit(solution)/shard_map/ppermute | solution.py:385
  45.7 11.5 %collective-permute-start.14 = (bf16[400,128]{1,0:T(8,128)(2,1)S(1)}, bf16[400,128]{1,0:T(8,128)(2,1)S(1)}, u32[]{:S(2)}, u32[]{:S(2)}) collective-permute-start(bf16[400,128]{1,0:T(8,128)(2,1)S(1)} %get-tuple-element.44), channel_id=1, source_target_pairs={{0,16},{8,24},{16,0},{24,8},{1,17},{9,25},{17,1},{25,9},{2,18},{10... | collective-permute-start | bytes 307208 | tf_op jit(solution)/shard_map/ppermute | solution.py:385
  50.7 6.6 %collective-permute-start.15 = (bf16[400,128]{1,0:T(8,128)(2,1)S(1)}, bf16[400,128]{1,0:T(8,128)(2,1)S(1)}, u32[]{:S(2)}, u32[]{:S(2)}) collective-permute-start(bf16[400,128]{1,0:T(8,128)(2,1)S(1)} %get-tuple-element.45), channel_id=1, source_target_pairs={{0,24},{8,16},{16,8},{24,0},{1,25},{9,17},{17,9},{25,1},{2,26},{10... | collective-permute-start | bytes 307208 | tf_op jit(solution)/shard_map/ppermute | solution.py:385
